TPU v7x, 32 devices: a whole 2x2x4 slice. The times are simulated.
32 devices in a mesh: groups: 2 (over y), space: 8 (over z, x), tm: 2 (over core).
Axes of the slice: x: 2, y: 2, z: 4, core: 2. Of those that a mesh axis runs over, the one named last changes fastest.
Arguments:
- base_latent: bfloat16 [64, 2, 12, 128], P(('groups', 'space'), 'tm'), parts along dimension 0, may hold values from -6 to 6
- cotangent: bfloat16 [64, 8, 48, 128], P(('groups', 'space'), 'tm'), parts along dimension 0, may hold values from -6 to 6
- w_spatial: bfloat16 [3, 3, 128, 128], replicated, may hold values from -0.1875 to 0.1875
- w_temporal: bfloat16 [5, 128, 128], replicated, may hold values from -0.25 to 0.25
Outputs:
- result: bfloat16 [64, 8, 48, 128], P(('groups', 'space'), 'tm'), parts along dimension 0
- grad_base: float32 [64, 2, 12, 128], P(('groups', 'space'), 'tm'), parts along dimension 0
- grad_spatial: float32 [6, 3, 128, 128], P('groups'), parts along dimension 0
- grad_temporal: float32 [10, 128, 128], P('groups'), parts along dimension 0
There are 2 independent parts, one for each index of `groups`. A program takes and returns all parts, laid end to end along the dimension named above; an argument that names none is the same for every part. Nothing has to cross between parts.
All inputs are finite; a program needn't handle non-finite values.
Results may differ from a plain program's by a relative error of at most 0.0064.
Values may be sent and summed in bfloat16 or wider, within the bound.
No kernel may reach another device: no remote copies, remote signals or barrier semaphores. Data moves between devices by JAX's collectives and lax.ppermute only.
A program may use at most 64 MiB of HBM per device.

v0:
```python
import jax
import jax.numpy as jnp
from jax import lax
from jax.sharding import PartitionSpec as P

FRAME_DILATION = 2


def shifted(value, axis, by):
    count = lax.axis_size(axis)
    pairs = [(i, i + by) for i in range(count) if 0 <= i + by < count]
    return lax.ppermute(value, axis, pairs)


def extended(cells, sides, width):
    for axis, dim in sides:
        count = lax.axis_size(axis)
        ends = count - 1
        head = lax.slice_in_dim(cells, 0, width, axis=dim)
        tail = lax.slice_in_dim(cells, cells.shape[dim] - width, cells.shape[dim], axis=dim)
        cells = jnp.concatenate(
            [
                lax.ppermute(tail, axis, [(i, (i + 1) % count) for i in range(ends)]),
                cells,
                lax.ppermute(head, axis, [((i + 1) % count, i) for i in range(ends)]),
            ],
            axis=dim,
        )
    return cells


def widen_cols(field):
    left_cols = jnp.concatenate([field[:, :, :1], field[:, :, :-1]], axis=2)
    right_cols = jnp.concatenate([field[:, :, 1:], field[:, :, -1:]], axis=2)
    phases = jnp.stack(
        [
            0.375 * left_cols + 0.625 * field,
            0.125 * left_cols + 0.875 * field,
            0.875 * field + 0.125 * right_cols,
            0.625 * field + 0.375 * right_cols,
        ],
        axis=3,
    )
    return phases.reshape(field.shape[0], field.shape[1], field.shape[2] * 4, field.shape[3])


def widen_rows(below_rows, middle, above_rows):
    phases = jnp.stack(
        [
            0.375 * below_rows + 0.625 * middle,
            0.125 * below_rows + 0.875 * middle,
            0.875 * middle + 0.125 * above_rows,
            0.625 * middle + 0.375 * above_rows,
        ],
        axis=2,
    )
    return phases.reshape(middle.shape[0], middle.shape[1] * 4, middle.shape[2], middle.shape[3])


def silu_slope(value):
    sigmoid_val = jax.nn.sigmoid(value)
    return sigmoid_val * (1.0 + value * (1.0 - sigmoid_val))


def conv_three(padded, weight, row_count, col_count, start):
    frame_count = padded.shape[0]
    channels = weight.shape[3]
    summed = jnp.zeros((frame_count * row_count * col_count, channels), jnp.float32)
    for tap_row in range(3):
        for tap_col in range(3):
            r0 = start - tap_row if start else tap_row
            c0 = start - tap_col if start else tap_col
            frame_window = padded[:, r0 : r0 + row_count, c0 : c0 + col_count].reshape(
                -1, padded.shape[3]
            )
            kernel = weight[tap_row, tap_col] if not start else weight[tap_row, tap_col].T
            summed = summed + jnp.dot(frame_window, kernel, preferred_element_type=jnp.float32)
    return summed.reshape(frame_count, row_count, col_count, channels)


def space_grads(padded, delta, row_count, col_count):
    flat = delta.reshape(-1, delta.shape[3])
    taps = []
    for tap_row in range(3):
        for tap_col in range(3):
            frame_window = padded[
                :, tap_row : tap_row + row_count, tap_col : tap_col + col_count
            ].reshape(-1, padded.shape[3])
            taps.append(
                lax.dot_general(
                    frame_window, flat, (((0,), (0,)), ((), ())), preferred_element_type=jnp.float32
                )
            )
    return jnp.stack(taps).reshape(3, 3, padded.shape[3], delta.shape[3])


def conv_time(frames_extended, weight, frame_count, reversed_order):
    channels = weight.shape[2]
    tensor_shape = frames_extended.shape
    summed = jnp.zeros((frame_count * tensor_shape[1] * tensor_shape[2], channels), jnp.float32)
    for kernel_tap in range(5):
        frame_offset = (
            (4 - kernel_tap) * FRAME_DILATION if reversed_order else kernel_tap * FRAME_DILATION
        )
        frame_window = frames_extended[frame_offset : frame_offset + frame_count].reshape(
            -1, tensor_shape[3]
        )
        kernel = weight[kernel_tap].T if reversed_order else weight[kernel_tap]
        summed = summed + jnp.dot(frame_window, kernel, preferred_element_type=jnp.float32)
    return summed.reshape(frame_count, tensor_shape[1], tensor_shape[2], channels)


def time_grads(frames_extended, delta, frame_count):
    flat = delta.reshape(-1, delta.shape[3])
    taps = []
    for kernel_tap in range(5):
        frame_window = frames_extended[
            kernel_tap * FRAME_DILATION : kernel_tap * FRAME_DILATION + frame_count
        ].reshape(-1, frames_extended.shape[3])
        taps.append(
            lax.dot_general(
                frame_window, flat, (((0,), (0,)), ((), ())), preferred_element_type=jnp.float32
            )
        )
    return jnp.stack(taps)


def shrink_base(grad_image, row_rank, row_devices, latent_shape):
    frame_count, low_rows, low_cols, channels = latent_shape
    _, col_pull = jax.vjp(
        widen_cols, jnp.zeros((frame_count, grad_image.shape[1], low_cols, channels), jnp.float32)
    )
    narrow = col_pull(grad_image)[0].reshape(frame_count, low_rows, 4, low_cols, channels)
    to_lower = 0.375 * narrow[:, :, 0] + 0.125 * narrow[:, :, 1]
    to_middle = (
        0.625 * narrow[:, :, 0]
        + 0.875 * narrow[:, :, 1]
        + 0.875 * narrow[:, :, 2]
        + 0.625 * narrow[:, :, 3]
    )
    to_upper = 0.125 * narrow[:, :, 2] + 0.375 * narrow[:, :, 3]
    from_above = shifted(to_lower, "tm", -1)
    from_below = shifted(to_upper, "tm", 1)
    next_lower = jnp.concatenate([to_lower[:, 1:], from_above], axis=1)
    prev_upper = jnp.concatenate([from_below, to_upper[:, :-1]], axis=1)
    edge_low = jnp.where(row_rank == 0, to_lower, jnp.zeros_like(to_lower))
    edge_high = jnp.where(row_rank == row_devices - 1, to_upper, jnp.zeros_like(to_upper))
    empty_rows = jnp.zeros((frame_count, low_rows - 1, low_cols, channels), jnp.float32)
    summed = to_middle + next_lower + prev_upper
    return (
        summed
        + jnp.concatenate([edge_low, empty_rows], axis=1)
        + jnp.concatenate([empty_rows, edge_high], axis=1)
    )


def local(base_latent, cotangent, w_spatial, w_temporal):
    row_rank = lax.axis_index("tm")
    row_devices = lax.axis_size("tm")
    padded_base = extended(base_latent, (("tm", 1),), 1)
    low_first = jnp.where(row_rank == 0, base_latent, padded_base[:, :1])
    high_last = jnp.where(row_rank == row_devices - 1, base_latent, padded_base[:, -1:])
    latent32 = base_latent.astype(jnp.float32)
    below_rows = jnp.concatenate([low_first, base_latent[:, :-1]], axis=1).astype(jnp.float32)
    above_rows = jnp.concatenate([base_latent[:, 1:], high_last], axis=1).astype(jnp.float32)
    upsampled = widen_cols(widen_rows(below_rows, latent32, above_rows)).astype(jnp.bfloat16)
    frame_count, row_count, col_count = (upsampled.shape[0], upsampled.shape[1], upsampled.shape[2])
    image_ext = extended(upsampled, (("tm", 1),), 1)
    padded = jnp.pad(image_ext, ((0, 0), (0, 0), (1, 1), (0, 0)))
    pre_one = conv_three(padded, w_spatial, row_count, col_count, 0)
    first_activation = jax.nn.silu(pre_one).astype(jnp.bfloat16)
    frames_extended = extended(first_activation, (("space", 0),), 2 * FRAME_DILATION)
    pre_two = conv_time(frames_extended, w_temporal, frame_count, False)
    result = (upsampled.astype(jnp.float32) + jax.nn.silu(pre_two)).astype(jnp.bfloat16)
    upstream = cotangent.astype(jnp.float32)
    second_gradient = (upstream * silu_slope(pre_two)).astype(jnp.bfloat16)
    temporal_local = time_grads(frames_extended, second_gradient, frame_count)
    grad_temporal = lax.psum(temporal_local, ("space", "tm"))
    gradient_extended = extended(second_gradient, (("space", 0),), 2 * FRAME_DILATION)
    back_one = conv_time(gradient_extended, w_temporal, frame_count, True)
    delta_one = (back_one * silu_slope(pre_one)).astype(jnp.bfloat16)
    spatial_local = space_grads(padded, delta_one, row_count, col_count)
    delta_rows = extended(delta_one, (("tm", 1),), 1)
    delta_pad = jnp.pad(delta_rows, ((0, 0), (0, 0), (1, 1), (0, 0)))
    grad_image = upstream + conv_three(delta_pad, w_spatial, row_count, col_count, 2)
    grad_base = shrink_base(grad_image, row_rank, row_devices, base_latent.shape)
    grad_spatial = lax.psum(spatial_local, ("space", "tm"))
    return (result, grad_base, grad_spatial, grad_temporal)


def solution(mesh):
    in_specs = (
        P(("groups", "space"), "tm", None, None),
        P(("groups", "space"), "tm", None, None),
        P(),
        P(),
    )
    out_specs = (
        P(("groups", "space"), "tm", None, None),
        P(("groups", "space"), "tm", None, None),
        P("groups", None, None, None),
        P("groups", None, None),
    )
    return jax.shard_map(local, mesh=mesh, in_specs=in_specs, out_specs=out_specs, check_vma=False)
```

profile of v0, /device:TPU:0, one launch (start us, length us, event | category | flops | bytes accessed | tf_op | source)
XLA Modules:
  0.0 162.9 jit_solution(3683068652345166377)
XLA Ops:
  7.2 0.8 copy.55
  8.0 2.4 %collective-permute-start = (bf16[4,1,12,128]{3,1,2,0:T(2,128)(2,1)S(1)}, bf16[4,1,12,128]{3,1,2,0:T(2,128)(2,1)S(1)}, u32[]{:S(2)}, u32[]{:S(2)}) collective-permute-start(bf16[4,1,12,128]{3,1,2,0:T(2,128)(2,1)S(1)} %copy.55), channel_id=1, source_target_pairs={{0,1},{2,3},{4,5},{6,7},{8,9},{10,11},{12,13},{14,15},{16,17},{18,... | collective-permute-start | bytes 36872 | tf_op jit(solution)/shard_map/ppermute | solution.py:23
  10.4 1.3 collective-permute-start.1
  11.7 1.8 %collective-permute-done.1 = bf16[4,1,12,128]{3,1,2,0:T(2,128)(2,1)S(1)} collective-permute-done((bf16[4,1,12,128]{3,1,2,0:T(2,128)(2,1)S(1)}, bf16[4,1,12,128]{3,1,2,0:T(2,128)(2,1)S(1)}, u32[]{:S(2)}, u32[]{:S(2)}) %collective-permute-start.1) | collective-permute-done | bytes 12320 | tf_op jit(solution)/shard_map/ppermute | solution.py:25
  14.4 2.1 %collective-permute-start.2 = (bf16[4,1,48,128]{3,2,1,0:T(8,128)(2,1)S(1)}, bf16[4,1,48,128]{3,2,1,0:T(8,128)(2,1)S(1)}, u32[]{:S(2)}, u32[]{:S(2)}) collective-permute-start(bf16[4,1,48,128]{3,2,1,0:T(8,128)(2,1)S(1)} %get-tuple-element.34), channel_id=1, source_target_pairs={{0,1},{2,3},{4,5},{6,7},{8,9},{10,11},{12,13},{14,15},{16,17},{18,... | collective-permute-start | bytes 147464 | tf_op jit(solution)/shard_map/ppermute | solution.py:23
  16.5 1.3 collective-permute-start.3
  17.8 1.8 %collective-permute-done.3 = bf16[4,1,48,128]{3,2,1,0:T(8,128)(2,1)S(1)} collective-permute-done((bf16[4,1,48,128]{3,2,1,0:T(8,128)(2,1)S(1)}, bf16[4,1,48,128]{3,2,1,0:T(8,128)(2,1)S(1)}, u32[]{:S(2)}, u32[]{:S(2)}) %collective-permute-start.3) | collective-permute-done | bytes 49184 | tf_op jit(solution)/shard_map/ppermute | solution.py:25
  19.9 0.8 copy-done
  21.3 0.2 convolution_add_fusion.16
  22.3 0.2 fusion
  22.7 4.2 %collective-permute-start.4 = (bf16[4,4,48,128]{3,2,1,0:T(8,128)(2,1)S(1)}, bf16[4,4,48,128]{3,2,1,0:T(8,128)(2,1)S(1)}, u32[]{:S(2)}, u32[]{:S(2)}) collective-permute-start(bf16[4,4,48,128]{3,2,1,0:T(8,128)(2,1)S(1)} %multiply_convert_fusion.3), channel_id=1, source_target_pairs={{0,2},{2,4},{4,6},{6,8},{8,10},{10,12},{12,14},{1,3},{3,5},{5,7},{... | collective-permute-start | bytes 589832 | tf_op jit(solution)/shard_map/ppermute | solution.py:23
  26.9 1.3 collective-permute-start.5
  28.2 0.2 fusion.35
  28.4 3.0 %collective-permute-done.4 = bf16[4,4,48,128]{3,2,1,0:T(8,128)(2,1)S(1)} collective-permute-done((bf16[4,4,48,128]{3,2,1,0:T(8,128)(2,1)S(1)}, bf16[4,4,48,128]{3,2,1,0:T(8,128)(2,1)S(1)}, u32[]{:S(2)}, u32[]{:S(2)}) %collective-permute-start.4) | collective-permute-done | bytes 196640 | tf_op jit(solution)/shard_map/ppermute | solution.py:23
  31.4 4.0 %collective-permute-done.5 = bf16[4,4,48,128]{3,2,1,0:T(8,128)(2,1)S(1)} collective-permute-done((bf16[4,4,48,128]{3,2,1,0:T(8,128)(2,1)S(1)}, bf16[4,4,48,128]{3,2,1,0:T(8,128)(2,1)S(1)}, u32[]{:S(2)}, u32[]{:S(2)}) %collective-permute-start.5) | collective-permute-done | bytes 196640 | tf_op jit(solution)/shard_map/ppermute | solution.py:25
  35.9 0.2 fusion.1
  36.1 0.2 fusion.2
  36.3 0.7 copy-done.1
  37.0 0.9 fusion.21
  37.9 1.3 collective-permute-start.6
  39.2 5.1 %collective-permute-start.7 = (bf16[4,4,48,128]{3,2,1,0:T(8,128)(2,1)S(1)}, bf16[4,4,48,128]{3,2,1,0:T(8,128)(2,1)S(1)}, u32[]{:S(2)}, u32[]{:S(2)}) collective-permute-start(bf16[4,4,48,128]{3,2,1,0:T(8,128)(2,1)S(1)} %get-tuple-element.10), channel_id=1, source_target_pairs={{0,2},{2,4},{4,6},{6,8},{8,10},{10,12},{12,14},{1,3},{3,5},{5,7},{... | collective-permute-start | bytes 589832 | tf_op jit(solution)/shard_map/ppermute | solution.py:23
  44.4 0.2 fusion.12
  44.6 0.3 fusion.7
  44.9 0.3 fusion.11
  45.1 0.2 fusion.46
  45.3 0.3 fusion.6
  45.6 0.3 fusion.10
  45.9 0.6 collective-permute-done.6
  46.5 5.2 %collective-permute-done.7 = bf16[4,4,48,128]{3,2,1,0:T(8,128)(2,1)S(1)} collective-permute-done((bf16[4,4,48,128]{3,2,1,0:T(8,128)(2,1)S(1)}, bf16[4,4,48,128]{3,2,1,0:T(8,128)(2,1)S(1)}, u32[]{:S(2)}, u32[]{:S(2)}) %collective-permute-start.7) | collective-permute-done | bytes 196640 | tf_op jit(solution)/shard_map/ppermute | solution.py:23
  51.7 0.2 fusion.49
  51.9 0.2 fusion.40
  52.1 0.2 fusion.3
  52.4 0.3 multiply_convert_fusion
  52.8 0.2 fusion.19
  53.1 0.2 fusion.9
  53.3 0.3 fusion.18
  53.6 0.2 fusion.17
  53.9 0.2 fusion.16
  54.1 0.3 fusion.15
  54.4 0.2 fusion.14
  54.6 1.9 %collective-permute-start.8 = (bf16[4,1,48,128]{3,2,1,0:T(8,128)(2,1)S(1)}, bf16[4,1,48,128]{3,2,1,0:T(8,128)(2,1)S(1)}, u32[]{:S(2)}, u32[]{:S(2)}) collective-permute-start(bf16[4,1,48,128]{3,2,1,0:T(8,128)(2,1)S(1)} %get-tuple-element.26), channel_id=1, source_target_pairs={{0,1},{2,3},{4,5},{6,7},{8,9},{10,11},{12,13},{14,15},{16,17},{18,... | collective-permute-start | bytes 147464 | tf_op jit(solution)/shard_map/ppermute | solution.py:23
  56.6 1.3 collective-permute-start.9
  57.9 0.3 fusion.8
  58.1 0.3 fusion.13
  58.4 0.8 copy-done.2
  59.2 0.5 collective-permute-done.9
  60.0 0.2 fusion.73
  60.2 0.2 convolution_add_fusion.6
  60.4 0.2 convolution_add_fusion.5
  60.7 0.2 convolution_add_fusion.4
  60.9 0.2 convolution_add_fusion.3
  61.1 0.2 fusion.55
  61.3 0.2 convolution_add_fusion.2
  61.5 0.2 convolution_add_fusion.1
  61.7 0.2 fusion.5
  62.0 0.3 fusion.122
  62.5 0.6 copy-done.7
  63.3 1.3 collective-permute-start.10
  64.6 3.0 %collective-permute-start.11 = (f32[4,1,12,128]{3,1,2,0:T(1,128)S(1)}, f32[4,1,12,128]{3,1,2,0:T(1,128)S(1)}, u32[]{:S(2)}, u32[]{:S(2)}) collective-permute-start(f32[4,1,12,128]{3,1,2,0:T(1,128)S(1)} %get-tuple-element.40), channel_id=1, source_target_pairs={{0,1},{2,3},{4,5},{6,7},{8,9},{10,11},{12,13},{14,15},{16,17},{18,... | collective-permute-start | bytes 73736 | tf_op jit(solution)/shard_map/ppermute | solution.py:12
  67.7 0.8 collective-permute-done.11
  68.5 0.7 fusion.107
  69.2 84.1 %all-reduce.8.cloned.1.call-done = (f32[3,3,128,128]{3,2,1,0:T(8,128)}, f32[5,128,128]{2,1,0:T(8,128)}) async-done(((f32[3,3,128,128]{3,2,1,0:T(8,128)}, f32[5,128,128]{2,1,0:T(8,128)}), (f32[3,3,128,128]{3,2,1,0:T(8,128)}, f32[5,128,128]{2,1,0:T(8,128)})) %all-reduce.8.cloned.1.call-update) | async-done | bytes 917520 | tf_op jit(solution)/shard_map/psum | solution.py:187
  153.4 2.0 %copy.127 = f32[3,3,128,128]{3,2,1,0:T(8,128)} copy(f32[3,3,128,128]{3,2,1,0:T(8,128)} %get-tuple-element.58) | data formatting | bytes 1179648
  155.3 0.7 copy.128
  (54 shorter events, 4.1 us)
Async XLA Ops:
  7.2 146.2 %all-reduce.8.cloned.1.call-start = ((), (), s32[]{:S(2)}) async-start(), calls=%async_computation | async-start | bytes 1835008 | tf_op jit(solution)/shard_map/psum | solution.py:187
  7.2 6.3 %copy-start.6 = (bf16[4,1,12,128]{3,0,2,1:T(4,128)(2,1)S(1)}, bf16[4,1,12,128]{3,0,2,1:T(4,128)(2,1)}, u32[]{:S(2)}) copy-start(bf16[4,1,12,128]{3,0,2,1:T(4,128)(2,1)} %param.4) | copy-start | bytes 36868
  8.0 3.7 %collective-permute-start = (bf16[4,1,12,128]{3,1,2,0:T(2,128)(2,1)S(1)}, bf16[4,1,12,128]{3,1,2,0:T(2,128)(2,1)S(1)}, u32[]{:S(2)}, u32[]{:S(2)}) collective-permute-start(bf16[4,1,12,128]{3,1,2,0:T(2,128)(2,1)S(1)} %copy.55), channel_id=1, source_target_pairs={{0,1},{2,3},{4,5},{6,7},{8,9},{10,11},{12,13},{14,15},{16,17},{18,... | collective-permute-start | bytes 36872 | tf_op jit(solution)/shard_map/ppermute | solution.py:23
  10.4 3.1 %collective-permute-start.1 = (bf16[4,1,12,128]{3,1,2,0:T(2,128)(2,1)S(1)}, bf16[4,1,12,128]{3,1,2,0:T(2,128)(2,1)S(1)}, u32[]{:S(2)}, u32[]{:S(2)}) collective-permute-start(bf16[4,1,12,128]{3,1,2,0:T(2,128)(2,1)S(1)} %copy.55), channel_id=1, source_target_pairs={{1,0},{3,2},{5,4},{7,6},{9,8},{11,10},{13,12},{15,14},{17,16},{19,... | collective-permute-start | bytes 36872 | tf_op jit(solution)/shard_map/ppermute | solution.py:25
  14.4 3.4 %collective-permute-start.2 = (bf16[4,1,48,128]{3,2,1,0:T(8,128)(2,1)S(1)}, bf16[4,1,48,128]{3,2,1,0:T(8,128)(2,1)S(1)}, u32[]{:S(2)}, u32[]{:S(2)}) collective-permute-start(bf16[4,1,48,128]{3,2,1,0:T(8,128)(2,1)S(1)} %get-tuple-element.34), channel_id=1, source_target_pairs={{0,1},{2,3},{4,5},{6,7},{8,9},{10,11},{12,13},{14,15},{16,17},{18,... | collective-permute-start | bytes 147464 | tf_op jit(solution)/shard_map/ppermute | solution.py:23
  16.5 3.1 %collective-permute-start.3 = (bf16[4,1,48,128]{3,2,1,0:T(8,128)(2,1)S(1)}, bf16[4,1,48,128]{3,2,1,0:T(8,128)(2,1)S(1)}, u32[]{:S(2)}, u32[]{:S(2)}) collective-permute-start(bf16[4,1,48,128]{3,2,1,0:T(8,128)(2,1)S(1)} %get-tuple-element.35), channel_id=1, source_target_pairs={{1,0},{3,2},{5,4},{7,6},{9,8},{11,10},{13,12},{15,14},{17,16},{19,... | collective-permute-start | bytes 147464 | tf_op jit(solution)/shard_map/ppermute | solution.py:25
  19.7 1.0 copy-start
  22.5 5.7 %copy-start.3 = (bf16[5,128,128]{2,1,0:T(8,128)(2,1)S(1)}, bf16[5,128,128]{2,1,0:T(8,128)(2,1)}, u32[]{:S(2)}) copy-start(bf16[5,128,128]{2,1,0:T(8,128)(2,1)} %param.7) | copy-start | bytes 491524
  22.7 8.8 %collective-permute-start.4 = (bf16[4,4,48,128]{3,2,1,0:T(8,128)(2,1)S(1)}, bf16[4,4,48,128]{3,2,1,0:T(8,128)(2,1)S(1)}, u32[]{:S(2)}, u32[]{:S(2)}) collective-permute-start(bf16[4,4,48,128]{3,2,1,0:T(8,128)(2,1)S(1)} %multiply_convert_fusion.3), channel_id=1, source_target_pairs={{0,2},{2,4},{4,6},{6,8},{8,10},{10,12},{12,14},{1,3},{3,5},{5,7},{... | collective-permute-start | bytes 589832 | tf_op jit(solution)/shard_map/ppermute | solution.py:23
  26.9 8.6 %collective-permute-start.5 = (bf16[4,4,48,128]{3,2,1,0:T(8,128)(2,1)S(1)}, bf16[4,4,48,128]{3,2,1,0:T(8,128)(2,1)S(1)}, u32[]{:S(2)}, u32[]{:S(2)}) collective-permute-start(bf16[4,4,48,128]{3,2,1,0:T(8,128)(2,1)S(1)} %multiply_convert_fusion.3), channel_id=1, source_target_pairs={{2,0},{4,2},{6,4},{8,6},{10,8},{12,10},{14,12},{3,1},{5,3},{7,5},{... | collective-permute-start | bytes 589832 | tf_op jit(solution)/shard_map/ppermute | solution.py:25
  36.1 0.9 copy-start.1
  37.9 8.5 %collective-permute-start.6 = (bf16[4,4,48,128]{3,2,1,0:T(8,128)(2,1)S(1)}, bf16[4,4,48,128]{3,2,1,0:T(8,128)(2,1)S(1)}, u32[]{:S(2)}, u32[]{:S(2)}) collective-permute-start(bf16[4,4,48,128]{3,2,1,0:T(8,128)(2,1)S(1)} %get-tuple-element.10), channel_id=1, source_target_pairs={{2,0},{4,2},{6,4},{8,6},{10,8},{12,10},{14,12},{3,1},{5,3},{7,5},{... | collective-permute-start | bytes 589832 | tf_op jit(solution)/shard_map/ppermute | solution.py:25
  39.2 12.4 %collective-permute-start.7 = (bf16[4,4,48,128]{3,2,1,0:T(8,128)(2,1)S(1)}, bf16[4,4,48,128]{3,2,1,0:T(8,128)(2,1)S(1)}, u32[]{:S(2)}, u32[]{:S(2)}) collective-permute-start(bf16[4,4,48,128]{3,2,1,0:T(8,128)(2,1)S(1)} %get-tuple-element.10), channel_id=1, source_target_pairs={{0,2},{2,4},{4,6},{6,8},{8,10},{10,12},{12,14},{1,3},{3,5},{5,7},{... | collective-permute-start | bytes 589832 | tf_op jit(solution)/shard_map/ppermute | solution.py:23
  45.9 5.8 %copy-start.4 = (f32[5,128,128]{2,1,0:T(8,128)}, f32[5,128,128]{2,1,0:T(8,128)S(1)}, u32[]{:S(2)}) copy-start(f32[5,128,128]{2,1,0:T(8,128)S(1)} %fusion.10) | copy-start | bytes 983044
  54.6 4.6 %collective-permute-start.8 = (bf16[4,1,48,128]{3,2,1,0:T(8,128)(2,1)S(1)}, bf16[4,1,48,128]{3,2,1,0:T(8,128)(2,1)S(1)}, u32[]{:S(2)}, u32[]{:S(2)}) collective-permute-start(bf16[4,1,48,128]{3,2,1,0:T(8,128)(2,1)S(1)} %get-tuple-element.26), channel_id=1, source_target_pairs={{0,1},{2,3},{4,5},{6,7},{8,9},{10,11},{12,13},{14,15},{16,17},{18,... | collective-permute-start | bytes 147464 | tf_op jit(solution)/shard_map/ppermute | solution.py:23
  56.6 3.1 %collective-permute-start.9 = (bf16[4,1,48,128]{3,2,1,0:T(8,128)(2,1)S(1)}, bf16[4,1,48,128]{3,2,1,0:T(8,128)(2,1)S(1)}, u32[]{:S(2)}, u32[]{:S(2)}) collective-permute-start(bf16[4,1,48,128]{3,2,1,0:T(8,128)(2,1)S(1)} %get-tuple-element.27), channel_id=1, source_target_pairs={{1,0},{3,2},{5,4},{7,6},{9,8},{11,10},{13,12},{15,14},{17,16},{19,... | collective-permute-start | bytes 147464 | tf_op jit(solution)/shard_map/ppermute | solution.py:25
  58.4 0.8 copy-start.2
  62.4 0.7 copy-start.7
  63.3 4.3 %collective-permute-start.10 = (f32[4,1,12,128]{3,1,2,0:T(1,128)S(1)}, f32[4,1,12,128]{3,1,2,0:T(1,128)S(1)}, u32[]{:S(2)}, u32[]{:S(2)}) collective-permute-start(f32[4,1,12,128]{3,1,2,0:T(1,128)S(1)} %get-tuple-element.41), channel_id=1, source_target_pairs={{1,0},{3,2},{5,4},{7,6},{9,8},{11,10},{13,12},{15,14},{17,16},{19,... | collective-permute-start | bytes 73736 | tf_op jit(solution)/shard_map/ppermute | solution.py:12
  64.6 3.9 %collective-permute-start.11 = (f32[4,1,12,128]{3,1,2,0:T(1,128)S(1)}, f32[4,1,12,128]{3,1,2,0:T(1,128)S(1)}, u32[]{:S(2)}, u32[]{:S(2)}) collective-permute-start(f32[4,1,12,128]{3,1,2,0:T(1,128)S(1)} %get-tuple-element.40), channel_id=1, source_target_pairs={{0,1},{2,3},{4,5},{6,7},{8,9},{10,11},{12,13},{14,15},{16,17},{18,... | collective-permute-start | bytes 73736 | tf_op jit(solution)/shard_map/ppermute | solution.py:12
  153.4 2.0 %copy-start.5 = (f32[5,128,128]{2,1,0:T(8,128)S(1)}, f32[5,128,128]{2,1,0:T(8,128)}, u32[]{:S(2)}) copy-start(f32[5,128,128]{2,1,0:T(8,128)} %get-tuple-element.59) | copy-start | bytes 983044
Sparse Core Ops, SparseCore 0:
  59.3 93.9 all-reduce.7
where the time goes:
time: 163 us
  waiting for transfers between devices  102 us (63%)
  starting transfers between devices  26.5 us (16%)
  between operations  14.7 us (9%)
  matrix products  9.25 us (6%)
  local copies, waits for them, and re-layouts  7.29 us (4%)
  other arithmetic  3.34 us (2%)
    psum x1, waiting for transfers between devices, local(): grad_spatial = lax.psum(spatial_local, ('space', 'tm'))  84.1 us
    ppermute x5, starting transfers between devices, extended(): lax.ppermute(tail, axis, [(i, (i + 1) % count) for i in range(ends)])  15.7 us
    ppermute x5, waiting for transfers between devices, extended(): lax.ppermute(head, axis, [((i + 1) % count, i) for i in range(ends)])  8.69 us
    ppermute x5, waiting for transfers between devices, extended(): lax.ppermute(tail, axis, [(i, (i + 1) % count) for i in range(ends)])  8.19 us
    ppermute x5, starting transfers between devices, extended(): lax.ppermute(head, axis, [((i + 1) % count, i) for i in range(ends)])  6.45 us
    unnamed x19, local copies, waits for them, and re-layouts  6.45 us
    ppermute x2, starting transfers between devices, shifted(): return lax.ppermute(value, axis, pairs)  4.32 us
    dot_general x18, matrix products, conv_three(): jnp.dot(frame_window, kernel, preferred_element_type=jnp.float32)  3.61 us
  transfers between devices with their start and end apart: 13, of which 9 were waited for; matrix products, arithmetic and copies ran while one was open for 4% of the time, Pallas kernels for 0%

commit v1 on v0

--- a/solution.py
+++ b/solution.py
@@ -184,7 +184,8 @@
     delta_pad = jnp.pad(delta_rows, ((0, 0), (0, 0), (1, 1), (0, 0)))
     grad_image = upstream + conv_three(delta_pad, w_spatial, row_count, col_count, 2)
     grad_base = shrink_base(grad_image, row_rank, row_devices, base_latent.shape)
-    grad_spatial = lax.psum(spatial_local, ("space", "tm"))
+    terms = lax.all_gather(spatial_local, ("space", "tm"))
+    grad_spatial = jnp.sum(terms, axis=0)
     return (result, grad_base, grad_spatial, grad_temporal)
 
 

time: 163 us -> 242 us (1.48)
  waiting for transfers between devices: 102 us -> 173 us
  other arithmetic: 3.34 us -> 9.22 us
  matrix products: 9.25 us -> 13 us
    all_gather x0 -> x1, waiting for transfers between devices: none -> 68.1 us  [local(): terms = lax.all_gather(spatial_local, ('space', 'tm'))]
    reduce_sum x0 -> x1, other arithmetic: none -> 5.18 us  [local(): grad_spatial = jnp.sum(terms, axis=0)]
    dot_general x18, matrix products: 3.61 us -> 7.41 us  [conv_three(): jnp.dot(frame_window, kernel, preferred_element_type=jnp.float32)]
    unnamed x19 -> x14, local copies, waits for them, and re-layouts: 6.45 us -> 4.03 us
  transfers between devices with their start and end apart: 13 -> 14, of which waited for: 9 -> 9; matrix products, arithmetic and copies ran while one was open for 4% -> 4% of each run, Pallas kernels for 0% -> 0%
where the time goes in v1:
time: 242 us; the launch traced here: 241 us
  waiting for transfers between devices  173 us (71%)
  starting transfers between devices  26.5 us (11%)
  between operations  14.7 us (6%)
  matrix products  13 us (5%)
  other arithmetic  9.22 us (4%)
  local copies, waits for them, and re-layouts  4.88 us (2%)
    psum x1, waiting for transfers between devices, local(): grad_temporal = lax.psum(temporal_local, ('space', 'tm'))  85.4 us
    all_gather x1, waiting for transfers between devices, local(): terms = lax.all_gather(spatial_local, ('space', 'tm'))  68.1 us
    ppermute x5, starting transfers between devices, extended(): lax.ppermute(tail, axis, [(i, (i + 1) % count) for i in range(ends)])  15.7 us
    ppermute x5, waiting for transfers between devices, extended(): lax.ppermute(head, axis, [((i + 1) % count, i) for i in range(ends)])  11.1 us
    ppermute x5, waiting for transfers between devices, extended(): lax.ppermute(tail, axis, [(i, (i + 1) % count) for i in range(ends)])  8.23 us
    dot_general x18, matrix products, conv_three(): jnp.dot(frame_window, kernel, preferred_element_type=jnp.float32)  7.41 us
    ppermute x5, starting transfers between devices, extended(): lax.ppermute(head, axis, [((i + 1) % count, i) for i in range(ends)])  6.45 us
    reduce_sum x1, other arithmetic, local(): grad_spatial = jnp.sum(terms, axis=0)  5.18 us
  transfers between devices with their start and end apart: 14, of which 9 were waited for; matrix products, arithmetic and copies ran while one was open for 4% of the time, Pallas kernels for 0%

profile of v1, /device:TPU:0, one launch (start us, length us, event | category | flops | bytes accessed | tf_op | source)
XLA Modules:
  0.0 241.2 jit_solution(15015682370104539081)
XLA Ops:
  7.2 0.8 copy.75
  8.0 2.4 collective-permute-start
  10.4 1.3 collective-permute-start.1
  11.7 1.8 collective-permute-done.1
  13.5 0.8 add_bitcast_fusion.7
  15.1 2.1 collective-permute-start.2
  17.2 1.3 collective-permute-start.3
  18.5 1.8 collective-permute-done.3
  20.6 0.9 fusion.75
  21.6 0.9 fusion.57
  22.6 1.0 convolution_add_fusion.17
  23.5 0.9 convolution_add_fusion.16
  24.5 1.0 convolution_add_fusion.15
  26.4 4.2 %collective-permute-start.4 = (bf16[4,4,48,128]{3,2,1,0:T(8,128)(2,1)S(1)}, bf16[4,4,48,128]{3,2,1,0:T(8,128)(2,1)S(1)}, u32[]{:S(2)}, u32[]{:S(2)}) collective-permute-start(bf16[4,4,48,128]{3,2,1,0:T(8,128)(2,1)S(1)} %multiply_convert_fusion.3), channel_id=1, source_target_pairs={{0,2},{2,4},{4,6},{6,8},{8,10},{10,12},{12,14},{1,3},{3,5},{5,7},{... | collective-permute-start | bytes 589832 | tf_op jit(solution)/shard_map/ppermute | solution.py:23
  30.6 1.3 collective-permute-start.5
  31.9 0.2 fusion.35
  32.1 3.0 %collective-permute-done.4 = bf16[4,4,48,128]{3,2,1,0:T(8,128)(2,1)S(1)} collective-permute-done((bf16[4,4,48,128]{3,2,1,0:T(8,128)(2,1)S(1)}, bf16[4,4,48,128]{3,2,1,0:T(8,128)(2,1)S(1)}, u32[]{:S(2)}, u32[]{:S(2)}) %collective-permute-start.4) | collective-permute-done | bytes 196640 | tf_op jit(solution)/shard_map/ppermute | solution.py:23
  35.1 4.0 %collective-permute-done.5 = bf16[4,4,48,128]{3,2,1,0:T(8,128)(2,1)S(1)} collective-permute-done((bf16[4,4,48,128]{3,2,1,0:T(8,128)(2,1)S(1)}, bf16[4,4,48,128]{3,2,1,0:T(8,128)(2,1)S(1)}, u32[]{:S(2)}, u32[]{:S(2)}) %collective-permute-start.5) | collective-permute-done | bytes 196640 | tf_op jit(solution)/shard_map/ppermute | solution.py:25
  40.0 0.9 fusion.21
  40.9 1.3 collective-permute-start.6
  42.2 5.1 %collective-permute-start.7 = (bf16[4,4,48,128]{3,2,1,0:T(8,128)(2,1)S(1)}, bf16[4,4,48,128]{3,2,1,0:T(8,128)(2,1)S(1)}, u32[]{:S(2)}, u32[]{:S(2)}) collective-permute-start(bf16[4,4,48,128]{3,2,1,0:T(8,128)(2,1)S(1)} %get-tuple-element.8), channel_id=1, source_target_pairs={{0,2},{2,4},{4,6},{6,8},{8,10},{10,12},{12,14},{1,3},{3,5},{5,7},{... | collective-permute-start | bytes 589832 | tf_op jit(solution)/shard_map/ppermute | solution.py:23
  47.3 0.2 fusion.46
  47.5 1.9 collective-permute-done.6
  49.4 5.2 %collective-permute-done.7 = bf16[4,4,48,128]{3,2,1,0:T(8,128)(2,1)S(1)} collective-permute-done((bf16[4,4,48,128]{3,2,1,0:T(8,128)(2,1)S(1)}, bf16[4,4,48,128]{3,2,1,0:T(8,128)(2,1)S(1)}, u32[]{:S(2)}, u32[]{:S(2)}) %collective-permute-start.7) | collective-permute-done | bytes 196640 | tf_op jit(solution)/shard_map/ppermute | solution.py:23
  54.7 0.2 fusion.49
  54.9 0.2 fusion.40
  55.1 0.2 fusion.3
  55.3 0.3 multiply_convert_fusion
  55.8 0.2 fusion.19
  56.0 0.2 fusion.9
  56.3 0.3 fusion.18
  56.5 0.2 fusion.17
  56.8 0.2 fusion.16
  57.1 0.3 fusion.15
  57.3 0.2 fusion.14
  57.6 0.2 fusion.8
  57.8 0.3 fusion.13
  58.1 0.8 copy-done.2
  59.0 0.3 fusion.12
  59.2 0.3 fusion.7
  59.5 0.3 fusion.11
  59.8 1.9 collective-permute-start.8
  61.7 1.3 collective-permute-start.9
  63.0 0.3 fusion.6
  63.3 1.6 collective-permute-done.9
  65.2 0.2 fusion.73
  65.4 0.2 fusion.55
  65.6 0.2 convolution_add_fusion.6
  65.8 0.2 convolution_add_fusion.5
  66.0 0.2 convolution_add_fusion.4
  66.2 0.2 convolution_add_fusion.3
  66.5 0.2 convolution_add_fusion.2
  66.7 0.2 convolution_add_fusion.1
  66.9 0.2 fusion.5
  67.2 0.3 fusion.122
  67.9 1.3 collective-permute-start.10
  69.2 3.0 %collective-permute-start.11 = (f32[4,1,12,128]{3,1,2,0:T(1,128)S(1)}, f32[4,1,12,128]{3,1,2,0:T(1,128)S(1)}, u32[]{:S(2)}, u32[]{:S(2)}) collective-permute-start(f32[4,1,12,128]{3,1,2,0:T(1,128)S(1)} %get-tuple-element.38), channel_id=1, source_target_pairs={{0,1},{2,3},{4,5},{6,7},{8,9},{10,11},{12,13},{14,15},{16,17},{18,... | collective-permute-start | bytes 73736 | tf_op jit(solution)/shard_map/ppermute | solution.py:12
  72.2 0.2 fusion.10
  72.5 0.7 copy-done.4
  73.2 0.7 fusion.107
  74.0 68.1 %all-gather.2.cloned.1.call-done = f32[16,3,3,128,128]{4,3,2,1,0:T(8,128)} async-done(((f32[1,3,3,128,128]{4,3,2,1,0:T(8,128)}), f32[16,3,3,128,128]{4,3,2,1,0:T(8,128)}) %all-gather.2.cloned.1.call-update) | async-done | bytes 9437200 | tf_op jit(solution)/shard_map/all_gather | solution.py:187
  142.1 5.2 %reduce_sum.9 = f32[3,3,128,128]{3,2,1,0:T(8,128)} reduce(f32[16,3,3,128,128]{4,3,2,1,0:T(8,128)} %all-gather.2.cloned.1.call-done, f32[]{:T(128)} %constant.9.clone.1), dimensions={0}, to_apply=%region_0.1 | reduce | flops 2211840 | bytes 10027012 | tf_op jit(solution)/shard_map/reduce_sum | solution.py:188
  147.2 85.4 %all-reduce.7.cloned.1.call-done = f32[5,128,128]{2,1,0:T(8,128)} async-done(((f32[5,128,128]{2,1,0:T(8,128)}), f32[5,128,128]{2,1,0:T(8,128)}) %all-reduce.7.cloned.1.call-update) | async-done | bytes 327696 | tf_op jit(solution)/shard_map/psum | solution.py:178
  232.6 1.7 copy.146
  (53 shorter events, 3.8 us)
Async XLA Ops:
  7.2 18.3 %copy-start = (bf16[3,3,128,128]{3,2,1,0:T(8,128)(2,1)S(1)}, bf16[3,3,128,128]{3,2,1,0:T(8,128)(2,1)}, u32[]{:S(2)}) copy-start(bf16[3,3,128,128]{3,2,1,0:T(8,128)(2,1)} %param.6) | copy-start | bytes 884740
  7.2 24.7 %copy-start.3 = (bf16[5,128,128]{2,1,0:T(8,128)(2,1)S(1)}, bf16[5,128,128]{2,1,0:T(8,128)(2,1)}, u32[]{:S(2)}) copy-start(bf16[5,128,128]{2,1,0:T(8,128)(2,1)} %param.7) | copy-start | bytes 491524
  7.2 134.9 %all-gather.2.cloned.1.call-start = ((), (), s32[]{:S(2)}) async-start(), calls=%async_computation | async-start | bytes 10027008 | tf_op jit(solution)/shard_map/all_gather | solution.py:187
  8.0 3.7 %collective-permute-start = (bf16[4,1,12,128]{3,1,2,0:T(2,128)(2,1)S(1)}, bf16[4,1,12,128]{3,1,2,0:T(2,128)(2,1)S(1)}, u32[]{:S(2)}, u32[]{:S(2)}) collective-permute-start(bf16[4,1,12,128]{3,1,2,0:T(2,128)(2,1)S(1)} %copy.75), channel_id=1, source_target_pairs={{0,1},{2,3},{4,5},{6,7},{8,9},{10,11},{12,13},{14,15},{16,17},{18,... | collective-permute-start | bytes 36872 | tf_op jit(solution)/shard_map/ppermute | solution.py:23
  10.4 3.1 %collective-permute-start.1 = (bf16[4,1,12,128]{3,1,2,0:T(2,128)(2,1)S(1)}, bf16[4,1,12,128]{3,1,2,0:T(2,128)(2,1)S(1)}, u32[]{:S(2)}, u32[]{:S(2)}) collective-permute-start(bf16[4,1,12,128]{3,1,2,0:T(2,128)(2,1)S(1)} %copy.75), channel_id=1, source_target_pairs={{1,0},{3,2},{5,4},{7,6},{9,8},{11,10},{13,12},{15,14},{17,16},{19,... | collective-permute-start | bytes 36872 | tf_op jit(solution)/shard_map/ppermute | solution.py:25
  15.1 3.4 %collective-permute-start.2 = (bf16[4,1,48,128]{3,2,1,0:T(8,128)(2,1)S(1)}, bf16[4,1,48,128]{3,2,1,0:T(8,128)(2,1)S(1)}, u32[]{:S(2)}, u32[]{:S(2)}) collective-permute-start(bf16[4,1,48,128]{3,2,1,0:T(8,128)(2,1)S(1)} %get-tuple-element.32), channel_id=1, source_target_pairs={{0,1},{2,3},{4,5},{6,7},{8,9},{10,11},{12,13},{14,15},{16,17},{18,... | collective-permute-start | bytes 147464 | tf_op jit(solution)/shard_map/ppermute | solution.py:23
  17.2 3.1 %collective-permute-start.3 = (bf16[4,1,48,128]{3,2,1,0:T(8,128)(2,1)S(1)}, bf16[4,1,48,128]{3,2,1,0:T(8,128)(2,1)S(1)}, u32[]{:S(2)}, u32[]{:S(2)}) collective-permute-start(bf16[4,1,48,128]{3,2,1,0:T(8,128)(2,1)S(1)} %get-tuple-element.33), channel_id=1, source_target_pairs={{1,0},{3,2},{5,4},{7,6},{9,8},{11,10},{13,12},{15,14},{17,16},{19,... | collective-permute-start | bytes 147464 | tf_op jit(solution)/shard_map/ppermute | solution.py:25
  20.4 19.6 %copy-start.1 = (bf16[4,4,48,128]{3,2,1,0:T(8,128)(2,1)S(1)}, bf16[4,4,48,128]{3,2,1,0:T(8,128)(2,1)}, u32[]{:S(2)}) copy-start(bf16[4,4,48,128]{3,2,1,0:T(8,128)(2,1)} %param.5) | copy-start | bytes 589828
  26.4 8.8 %collective-permute-start.4 = (bf16[4,4,48,128]{3,2,1,0:T(8,128)(2,1)S(1)}, bf16[4,4,48,128]{3,2,1,0:T(8,128)(2,1)S(1)}, u32[]{:S(2)}, u32[]{:S(2)}) collective-permute-start(bf16[4,4,48,128]{3,2,1,0:T(8,128)(2,1)S(1)} %multiply_convert_fusion.3), channel_id=1, source_target_pairs={{0,2},{2,4},{4,6},{6,8},{8,10},{10,12},{12,14},{1,3},{3,5},{5,7},{... | collective-permute-start | bytes 589832 | tf_op jit(solution)/shard_map/ppermute | solution.py:23
  30.6 8.6 %collective-permute-start.5 = (bf16[4,4,48,128]{3,2,1,0:T(8,128)(2,1)S(1)}, bf16[4,4,48,128]{3,2,1,0:T(8,128)(2,1)S(1)}, u32[]{:S(2)}, u32[]{:S(2)}) collective-permute-start(bf16[4,4,48,128]{3,2,1,0:T(8,128)(2,1)S(1)} %multiply_convert_fusion.3), channel_id=1, source_target_pairs={{2,0},{4,2},{6,4},{8,6},{10,8},{12,10},{14,12},{3,1},{5,3},{7,5},{... | collective-permute-start | bytes 589832 | tf_op jit(solution)/shard_map/ppermute | solution.py:25
  40.9 8.5 %collective-permute-start.6 = (bf16[4,4,48,128]{3,2,1,0:T(8,128)(2,1)S(1)}, bf16[4,4,48,128]{3,2,1,0:T(8,128)(2,1)S(1)}, u32[]{:S(2)}, u32[]{:S(2)}) collective-permute-start(bf16[4,4,48,128]{3,2,1,0:T(8,128)(2,1)S(1)} %get-tuple-element.8), channel_id=1, source_target_pairs={{2,0},{4,2},{6,4},{8,6},{10,8},{12,10},{14,12},{3,1},{5,3},{7,5},{... | collective-permute-start | bytes 589832 | tf_op jit(solution)/shard_map/ppermute | solution.py:25
  42.2 12.4 %collective-permute-start.7 = (bf16[4,4,48,128]{3,2,1,0:T(8,128)(2,1)S(1)}, bf16[4,4,48,128]{3,2,1,0:T(8,128)(2,1)S(1)}, u32[]{:S(2)}, u32[]{:S(2)}) collective-permute-start(bf16[4,4,48,128]{3,2,1,0:T(8,128)(2,1)S(1)} %get-tuple-element.8), channel_id=1, source_target_pairs={{0,2},{2,4},{4,6},{6,8},{8,10},{10,12},{12,14},{1,3},{3,5},{5,7},{... | collective-permute-start | bytes 589832 | tf_op jit(solution)/shard_map/ppermute | solution.py:23
  58.1 0.8 copy-start.2
  58.1 9.5 %copy-start.5 = (pred[12]{0:T(512)(128)(4,1)S(1)}, pred[12]{0:T(512)(128)(4,1)}, u32[]{:S(2)}) copy-start(pred[12]{0:T(512)(128)(4,1)} %constant.10.clone.1) | copy-start | bytes 40
  58.9 173.7 %all-reduce.7.cloned.1.call-start = ((), (), s32[]{:S(2)}) async-start(), calls=%async_computation.1 | async-start | bytes 655360 | tf_op jit(solution)/shard_map/psum | solution.py:178
  59.8 3.5 %collective-permute-start.8 = (bf16[4,1,48,128]{3,2,1,0:T(8,128)(2,1)S(1)}, bf16[4,1,48,128]{3,2,1,0:T(8,128)(2,1)S(1)}, u32[]{:S(2)}, u32[]{:S(2)}) collective-permute-start(bf16[4,1,48,128]{3,2,1,0:T(8,128)(2,1)S(1)} %get-tuple-element.24), channel_id=1, source_target_pairs={{0,1},{2,3},{4,5},{6,7},{8,9},{10,11},{12,13},{14,15},{16,17},{18,... | collective-permute-start | bytes 147464 | tf_op jit(solution)/shard_map/ppermute | solution.py:23
  61.7 3.1 %collective-permute-start.9 = (bf16[4,1,48,128]{3,2,1,0:T(8,128)(2,1)S(1)}, bf16[4,1,48,128]{3,2,1,0:T(8,128)(2,1)S(1)}, u32[]{:S(2)}, u32[]{:S(2)}) collective-permute-start(bf16[4,1,48,128]{3,2,1,0:T(8,128)(2,1)S(1)} %get-tuple-element.25), channel_id=1, source_target_pairs={{1,0},{3,2},{5,4},{7,6},{9,8},{11,10},{13,12},{15,14},{17,16},{19,... | collective-permute-start | bytes 147464 | tf_op jit(solution)/shard_map/ppermute | solution.py:25
  67.9 5.3 %collective-permute-start.10 = (f32[4,1,12,128]{3,1,2,0:T(1,128)S(1)}, f32[4,1,12,128]{3,1,2,0:T(1,128)S(1)}, u32[]{:S(2)}, u32[]{:S(2)}) collective-permute-start(f32[4,1,12,128]{3,1,2,0:T(1,128)S(1)} %get-tuple-element.39), channel_id=1, source_target_pairs={{1,0},{3,2},{5,4},{7,6},{9,8},{11,10},{13,12},{15,14},{17,16},{19,... | collective-permute-start | bytes 73736 | tf_op jit(solution)/shard_map/ppermute | solution.py:12
  69.2 4.1 %collective-permute-start.11 = (f32[4,1,12,128]{3,1,2,0:T(1,128)S(1)}, f32[4,1,12,128]{3,1,2,0:T(1,128)S(1)}, u32[]{:S(2)}, u32[]{:S(2)}) collective-permute-start(f32[4,1,12,128]{3,1,2,0:T(1,128)S(1)} %get-tuple-element.38), channel_id=1, source_target_pairs={{0,1},{2,3},{4,5},{6,7},{8,9},{10,11},{12,13},{14,15},{16,17},{18,... | collective-permute-start | bytes 73736 | tf_op jit(solution)/shard_map/ppermute | solution.py:12
  72.4 0.7 copy-start.4
Sparse Core Ops, SparseCore 0:
  59.1 82.9 all-gather.1
  146.0 86.5 all-reduce.6
